TPU v7x, 128 devices: a whole 4x4x4 slice. The times are simulated.
128 devices in a mesh: replica: 4 (over z), shard: 16 (over y, x_lo, core), tensor: 2 (over x_hi).
Axes of the slice: x: 4 (x_hi: 2, x_lo: 2; x = x_hi * 2 + x_lo), y: 4, z: 4, core: 2. Of those that a mesh axis runs over, the one named last changes fastest.
Arguments:
- trained_up: bfloat16 [4, 1024, 4096], P('replica', None, 'tensor'), may hold values from -6 to 6
- trained_down: bfloat16 [4, 4096, 1024], P('replica', 'tensor'), may hold values from -6 to 6
- trained_embed: bfloat16 [4, 32768, 1024], P('replica', ('shard', 'tensor')), may hold values from -6 to 6
- trained_norm: bfloat16 [4, 2, 1024], P('replica'), may hold values from 0.099609375 to 1.8984375
- master_up: float32 [1024, 4096], P(('replica', 'shard', 'tensor')), may hold values from -6 to 6
- moment_up: float32 [1024, 4096], P(('replica', 'shard', 'tensor')), may hold values from -4 to 4
- master_down: float32 [2, 2048, 1024], P('tensor', ('replica', 'shard')), may hold values from -6 to 6
- moment_down: float32 [2, 2048, 1024], P('tensor', ('replica', 'shard')), may hold values from -4 to 4
- master_embed: float32 [32, 1024, 1024], P(('shard', 'tensor'), 'replica'), may hold values from -6 to 6
- moment_embed: float32 [32, 1024, 64], P(('shard', 'tensor'), 'replica'), may hold values from -4 to 4
- master_norm: float32 [2, 1024], replicated, may hold values from 0.1 to 1.9
- moment_norm: float32 [2, 1024], replicated, may hold values from -2 to 2
- embed_basis: float32 [1024, 64], replicated, may hold values from -0.1875 to 0.1875
Outputs:
- recast_up: bfloat16 [1024, 4096], P(None, 'tensor')
- recast_down: bfloat16 [4096, 1024], P('tensor')
- recast_embed: bfloat16 [32768, 1024], P(('shard', 'tensor'))
- recast_norm: bfloat16 [2, 1024], replicated
- stored_up: float32 [1024, 4096], P(('replica', 'shard', 'tensor'))
- velocity_up: float32 [1024, 4096], P(('replica', 'shard', 'tensor'))
- stored_down: float32 [2, 2048, 1024], P('tensor', ('replica', 'shard'))
- velocity_down: float32 [2, 2048, 1024], P('tensor', ('replica', 'shard'))
- stored_embed: float32 [32, 1024, 1024], P(('shard', 'tensor'), 'replica')
- velocity_embed: float32 [32, 1024, 64], P(('shard', 'tensor'), 'replica')
- stored_norm: float32 [2, 1024], replicated
- velocity_norm: float32 [2, 1024], replicated
All inputs are finite; a program needn't handle non-finite values.
Results may differ from a plain program's by a relative error of at most 0.012.
Values may be sent and summed in bfloat16 or wider, within the bound.
A program may use at most 128 MiB of HBM per device.

v0:
```python
import jax
import jax.numpy as jnp
from jax import lax
from jax.sharding import PartitionSpec as P


def outer_step(master, moment, summed, groups):
    difference = master - summed / groups
    velocity = 0.5 * moment + difference
    return (master - 0.7 * (difference + 0.5 * velocity), velocity)


def body(
    trained_up,
    trained_down,
    trained_embed,
    trained_norm,
    master_up,
    moment_up,
    master_down,
    moment_down,
    master_embed,
    moment_embed,
    master_norm,
    moment_norm,
    embed_basis,
):
    replicas = lax.axis_size("replica")
    shards = lax.axis_size("shard")
    tensors = lax.axis_size("tensor")
    shard_pos = lax.axis_index("shard")
    width = embed_basis.shape[0]
    rows_up = master_up.shape[0]
    half_cols = trained_up.shape[2]
    rows_down = master_down.shape[1]
    up_blocks = trained_up[0].reshape(replicas, shards, tensors, rows_up, half_cols)
    up_own = lax.dynamic_index_in_dim(up_blocks, shard_pos, 1, keepdims=False)
    down_blocks = trained_down[0].reshape(replicas, shards, rows_down, width)
    down_own = lax.dynamic_index_in_dim(down_blocks, shard_pos, 1, keepdims=False)
    up_summed, down_summed = (
        lax.psum_scatter(
            up_own.astype(jnp.float32).astype(jnp.bfloat16),
            "replica",
            scatter_dimension=0,
            tiled=True,
        ).astype(jnp.float32),
        lax.psum_scatter(
            down_own.astype(jnp.float32).astype(jnp.bfloat16),
            "replica",
            scatter_dimension=0,
            tiled=True,
        ).astype(jnp.float32),
    )
    up_summed = lax.all_to_all(up_summed, "tensor", split_axis=1, concat_axis=3, tiled=True)
    stored_up, velocity_up = outer_step(
        master_up, moment_up, up_summed.reshape(rows_up, half_cols * tensors), replicas
    )
    stored_down, velocity_down = outer_step(master_down, moment_down, down_summed, replicas)
    norm_summed = lax.psum(trained_norm[0].astype(jnp.float32), "replica")
    stored_norm, velocity_norm = outer_step(master_norm, moment_norm, norm_summed, replicas)
    embed_own = master_embed[0]
    rows_embed = embed_own.shape[0]
    embed_terms = trained_embed[0].reshape(replicas, rows_embed, width).astype(jnp.float32)
    embed_summed = lax.psum_scatter(
        embed_terms.astype(jnp.bfloat16), "replica", scatter_dimension=0, tiled=True
    ).astype(jnp.float32)[0]
    coefficient = jnp.dot(
        embed_own - embed_summed / replicas, embed_basis, precision=lax.Precision.HIGHEST
    )
    velocity_rows = 0.5 * moment_embed[0] + coefficient
    stored_rows = embed_own - 0.7 * jnp.dot(
        coefficient + 0.5 * velocity_rows, embed_basis.T, precision=lax.Precision.HIGHEST
    )
    up_piece = lax.all_to_all(
        stored_up.astype(jnp.bfloat16), "tensor", split_axis=1, concat_axis=0, tiled=True
    )
    down_piece = stored_down[0].astype(jnp.bfloat16)
    recast_up, recast_down = (
        lax.all_gather(up_piece, ("replica", "shard"), axis=0, tiled=True),
        lax.all_gather(down_piece, ("replica", "shard"), axis=0, tiled=True),
    )
    recast_embed = lax.all_gather(stored_rows.astype(jnp.bfloat16), "replica", axis=0, tiled=True)
    return (
        recast_up,
        recast_down,
        recast_embed,
        stored_norm.astype(jnp.bfloat16),
        stored_up,
        velocity_up,
        stored_down,
        velocity_down,
        stored_rows[None],
        velocity_rows[None],
        stored_norm,
        velocity_norm,
    )


def solution(mesh):
    in_specs = (
        P("replica", None, "tensor"),
        P("replica", "tensor", None),
        P("replica", ("shard", "tensor"), None),
        P("replica", None, None),
        P(("replica", "shard", "tensor"), None),
        P(("replica", "shard", "tensor"), None),
        P("tensor", ("replica", "shard"), None),
        P("tensor", ("replica", "shard"), None),
        P(("shard", "tensor"), "replica", None),
        P(("shard", "tensor"), "replica", None),
        P(),
        P(),
        P(),
    )
    out_specs = (
        P(None, "tensor"),
        P("tensor", None),
        P(("shard", "tensor"), None),
        P(),
        P(("replica", "shard", "tensor"), None),
        P(("replica", "shard", "tensor"), None),
        P("tensor", ("replica", "shard"), None),
        P("tensor", ("replica", "shard"), None),
        P(("shard", "tensor"), "replica", None),
        P(("shard", "tensor"), "replica", None),
        P(),
        P(),
    )
    return jax.shard_map(body, mesh=mesh, in_specs=in_specs, out_specs=out_specs, check_vma=False)
```

profile of v0, /device:TPU:1, one launch (start us, length us, event | category | flops | bytes accessed | tf_op | source)
XLA Modules:
  0.0 376.6 jit_solution(8853071086595991756)
XLA Ops:
  7.2 0.0 reduce-scatter.6.cloned.1.call-start
  7.3 0.7 reduce-scatter.6.cloned.1.call-update
  8.0 0.0 all-reduce.3.cloned.1.call-start
  8.0 1.7 copy_bitcast_fusion
  9.7 0.0 reduce-scatter.4.cloned.1.call-start
  9.8 1.7 dynamic-slice_bitcast_fusion
  11.5 0.0 all-gather.7.cloned.1.call-start
  11.6 32.1 %reduce-scatter.6.cloned.1.call-done = bf16[1,256,1024]{2,1,0:T(8,128)(2,1)} async-done(((bf16[4,256,1024]{2,1,0:T(8,128)(2,1)}), bf16[1,256,1024]{2,1,0:T(8,128)(2,1)}) %reduce-scatter.6.cloned.1.call-update) | async-done | bytes 524304 | tf_op jit(solution)/shard_map/reduce_scatter | solution.py:64
  43.6 2.2 fusion.1
  45.8 2.2 fusion.16
  48.0 0.0 all-gather.7.cloned.1.call-update
  48.1 0.0 all-gather.5.cloned.1.call-start
  48.1 0.6 dynamic-slice
  48.7 37.3 %all-reduce.3.cloned.1.call-done = bf16[4,2,8,2048]{3,2,0,1:T(8,128)(2,1)} async-done(((bf16[4,2,8,2048]{3,2,0,1:T(8,128)(2,1)}), bf16[4,2,8,2048]{3,2,0,1:T(8,128)(2,1)}) %all-reduce.3.cloned.1.call-update) | async-done | bytes 262160
  86.0 1.5 dynamic-slice_convert_fusion
  87.5 8.6 %all_to_all.28 = f32[1,2,8,2048]{3,2,0,1:T(8,128)S(1)} all-to-all(f32[1,2,8,2048]{3,2,0,1:T(8,128)S(1)} %dynamic-slice_convert_fusion), channel_id=1, replica_groups=mesh['replica'=4,'shard'=16,'tensor'=2] {'tensor'}, dimensions={1} | all-to-all | bytes 262144 | tf_op jit(solution)/shard_map/all_to_all | solution.py:54
  96.1 0.7 fusion.15
  96.9 7.5 %all_to_all.29 = bf16[8,2,2048]{2,0,1:T(8,128)(2,1)} all-to-all(bf16[8,2,2048]{2,0,1:T(8,128)(2,1)S(1)} %bitcast.53), channel_id=1, replica_groups=mesh['replica'=4,'shard'=16,'tensor'=2] {'tensor'}, dimensions={1} | all-to-all | bytes 131072 | tf_op jit(solution)/shard_map/all_to_all | solution.py:74
  104.4 0.0 all-gather.5.cloned.1.call-update
  104.4 0.0 all-gather.9.cloned.1.call-start
  104.4 5.8 %reduce-scatter.4.cloned.1.call-done = bf16[1,32,1024]{2,1,0:T(8,128)(2,1)} async-done(((bf16[4,32,1024]{2,1,0:T(8,128)(2,1)}), bf16[1,32,1024]{2,1,0:T(8,128)(2,1)}) %reduce-scatter.4.cloned.1.call-update) | async-done | bytes 65552 | tf_op jit(solution)/shard_map/reduce_scatter | solution.py:47
  110.3 1.6 fusion.14
  111.9 6.9 %psum.7 = f32[2,1024]{1,0:T(2,128)S(1)} all-reduce(f32[2,1024]{1,0:T(2,128)S(1)} %bitcast_convert_fusion), channel_id=1, replica_groups=mesh['replica'=4,'shard'=16,'tensor'=2] {'replica'}, use_global_device_ids=true, to_apply=%region_3.4 | all-reduce | flops 2048 | bytes 16384 | tf_op jit(solution)/shard_map/psum | solution.py:59
  118.9 0.6 fusion.13
  119.5 0.6 fusion.8
  120.2 25.0 %all-gather.7.cloned.1.call-done = bf16[1024,1024]{1,0:T(8,128)(2,1)} async-done(((bf16[256,1024]{1,0:T(8,128)(2,1)}), bf16[1024,1024]{1,0:T(8,128)(2,1)}) %all-gather.7.cloned.1.call-update) | async-done | bytes 2097168 | tf_op jit(solution)/shard_map/all_gather | solution.py:82
  145.2 108.0 %all-gather.5.cloned.1.call-done = bf16[1024,2048]{1,0:T(8,128)(2,1)} async-done(((bf16[16,2048]{1,0:T(8,128)(2,1)}), bf16[1024,2048]{1,0:T(8,128)(2,1)}) %all-gather.5.cloned.1.call-update) | async-done | bytes 4194320 | tf_op jit(solution)/shard_map/all_gather | solution.py:79
  253.2 107.3 %all-gather.9.cloned.1.call-done = bf16[1,2048,1024]{2,1,0:T(8,128)(2,1)} async-done(((bf16[1,32,1024]{2,1,0:T(8,128)(2,1)}), bf16[1,2048,1024]{2,1,0:T(8,128)(2,1)}) %all-gather.9.cloned.1.call-update) | async-done | bytes 4194320 | tf_op jit(solution)/shard_map/all_gather | solution.py:80
  360.4 4.9 %copy.39 = bf16[1024,2048]{1,0:T(8,128)(2,1)} copy(bf16[1024,2048]{1,0:T(8,128)(2,1)} %all-gather.5.cloned.1.call-done) | data formatting | bytes 8388608
  365.4 2.1 copy.40
  367.5 1.0 copy-done.3
  368.5 1.3 copy.41
  (30 shorter events, 0.1 us)
Async XLA Ops:
  7.2 36.5 %copy-start = (f32[1024,64]{0,1:T(8,128)S(1)}, f32[1024,64]{0,1:T(8,128)}, u32[]{:S(2)}) copy-start(f32[1024,64]{0,1:T(8,128)} %param.25) | copy-start | bytes 786436
  7.2 36.5 %copy-start.1 = (f32[1,256,1024]{2,1,0:T(8,128)S(1)}, f32[1,256,1024]{2,1,0:T(8,128)}, u32[]{:S(2)}) copy-start(f32[1,256,1024]{2,1,0:T(8,128)} %param.21) | copy-start | bytes 3145732
  7.2 38.6 %copy-start.4 = (f32[1,256,64]{1,2,0:T(8,128)S(1)}, f32[1,256,64]{1,2,0:T(8,128)}, u32[]{:S(2)}) copy-start(f32[1,256,64]{1,2,0:T(8,128)} %param.22) | copy-start | bytes 196612
  7.2 36.4 %reduce-scatter.6.cloned.1.call-start = ((), (), s32[]{:S(2)}) async-start(), calls=%async_computation.6 | async-start | bytes 2621440 | tf_op jit(solution)/shard_map/reduce_scatter | solution.py:64
  7.3 40.9 %copy-start.12 = (u32[128]{0:T(128)S(1)}, u32[128]{0:T(128)}, u32[]{:S(2)}) copy-start(u32[128]{0:T(128)} %constant.47) | copy-start | bytes 1540
  7.9 88.2 %copy-start.7 = (f32[8,4096]{1,0:T(8,128)S(1)}, f32[8,4096]{1,0:T(8,128)}, u32[]{:S(2)}) copy-start(f32[8,4096]{1,0:T(8,128)} %param.17) | copy-start | bytes 393220
  8.0 88.2 %copy-start.8 = (f32[8,4096]{1,0:T(8,128)S(1)}, f32[8,4096]{1,0:T(8,128)}, u32[]{:S(2)}) copy-start(f32[8,4096]{1,0:T(8,128)} %param.18) | copy-start | bytes 393220
  8.0 78.0 %all-reduce.3.cloned.1.call-start = ((), (), s32[]{:S(2)}) async-start(), calls=%async_computation.9 | async-start | bytes 524288
  9.7 100.6 %copy-start.5 = (f32[1,32,1024]{2,1,0:T(8,128)S(1)}, f32[1,32,1024]{2,1,0:T(8,128)}, u32[]{:S(2)}) copy-start(f32[1,32,1024]{2,1,0:T(8,128)} %param.19) | copy-start | bytes 393220
  9.7 100.6 %copy-start.6 = (f32[1,32,1024]{2,1,0:T(8,128)S(1)}, f32[1,32,1024]{2,1,0:T(8,128)}, u32[]{:S(2)}) copy-start(f32[1,32,1024]{2,1,0:T(8,128)} %param.20) | copy-start | bytes 393220
  9.7 100.6 %reduce-scatter.4.cloned.1.call-start = ((), (), s32[]{:S(2)}) async-start(), calls=%async_computation.5 | async-start | bytes 327680 | tf_op jit(solution)/shard_map/reduce_scatter | solution.py:47
  9.8 102.1 %copy-start.11 = (bf16[1,2,1024]{2,1,0:T(2,128)(2,1)S(1)}, bf16[1,2,1024]{2,1,0:T(2,128)(2,1)}, u32[]{:S(2)}) copy-start(bf16[1,2,1024]{2,1,0:T(2,128)(2,1)} %param.16) | copy-start | bytes 12292
  11.5 107.4 %copy-start.9 = (f32[2,1024]{1,0:T(2,128)S(1)}, f32[2,1024]{1,0:T(2,128)}, u32[]{:S(2)}) copy-start(f32[2,1024]{1,0:T(2,128)} %param.23) | copy-start | bytes 24580
  11.5 107.4 %copy-start.10 = (f32[2,1024]{1,0:T(2,128)S(1)}, f32[2,1024]{1,0:T(2,128)}, u32[]{:S(2)}) copy-start(f32[2,1024]{1,0:T(2,128)} %param.24) | copy-start | bytes 24580
  11.5 133.6 %all-gather.7.cloned.1.call-start = ((), (), s32[]{:S(2)}) async-start(), calls=%async_computation.7 | async-start | bytes 2621440 | tf_op jit(solution)/shard_map/all_gather | solution.py:82
  48.1 205.1 %all-gather.5.cloned.1.call-start = ((), (), s32[]{:S(2)}) async-start(), calls=%async_computation.4 | async-start | bytes 4259840 | tf_op jit(solution)/shard_map/all_gather | solution.py:79
  104.4 256.0 %all-gather.9.cloned.1.call-start = ((), (), s32[]{:S(2)}) async-start(), calls=%async_computation.8 | async-start | bytes 4259840 | tf_op jit(solution)/shard_map/all_gather | solution.py:80
  360.4 4.9 %copy-start.2 = (bf16[1,2048,1024]{2,1,0:T(8,128)(2,1)S(1)}, bf16[1,2048,1024]{2,1,0:T(8,128)(2,1)}, u32[]{:S(2)}) copy-start(bf16[1,2048,1024]{2,1,0:T(8,128)(2,1)} %all-gather.9.cloned.1.call-done) | copy-start | bytes 12582916
  365.4 3.1 copy-start.3
Sparse Core Ops, SparseCore 0:
  10.4 33.1 reduce-scatter.5
  46.7 39.3 all-reduce.2
  89.0 21.2 reduce-scatter.3
  112.5 32.6 all-gather.6
  146.9 106.2 all-gather.4
  255.4 104.9 all-gather.8
where the time goes:
time: 377 us
  waiting for transfers between devices  316 us (84%)
  blocking collectives  23 us (6%)
  between operations  14.3 us (4%)
  local copies, waits for them, and re-layouts  13.4 us (4%)
  other arithmetic  5.09 us (1%)
  matrix products  4.38 us (1%)
    all_gather x1, waiting for transfers between devices, body(): lax.all_gather(up_piece, ('replica', 'shard'), axis=0, tiled=True)  108 us
    all_gather x1, waiting for transfers between devices, body(): lax.all_gather(down_piece, ('replica', 'shard'), axis=0, tiled=True)  107 us
    unnamed x7, waiting for transfers between devices  38.1 us
    reduce_scatter x1, waiting for transfers between devices, body(): lax.psum_scatter(embed_terms.astype(jnp.bfloat16), 'replica', scatter_dim...  32.1 us
    all_gather x1, waiting for transfers between devices, body(): lax.all_gather(stored_rows.astype(jnp.bfloat16), 'replica', axis=0, tiled...  25 us
    unnamed x30, local copies, waits for them, and re-layouts  10 us
    all_to_all x1, blocking collectives, body(): lax.all_to_all(up_summed, 'tensor', split_axis=1, concat_axis=3, tiled=True)  8.59 us
  transfers between devices with their start and end apart: 6, of which 6 were waited for; matrix products, arithmetic and copies ran while one was open for 4% of the time, Pallas kernels for 0%

commit v1 on v0

--- a/solution.py
+++ b/solution.py
@@ -2,6 +2,34 @@
 import jax.numpy as jnp
 from jax import lax
 from jax.sharding import PartitionSpec as P
+
+
+def _pack_boxes(z_in, which_axis):
+    g_now, newest, shaped = (lax.axis_size(which_axis), lax.axis_index(which_axis), z_in.shape[0])
+    lanes = []
+    for it, ix in enumerate(z_in.shape):
+        lanes.append(ix * g_now if it == 0 else ix)
+    current_block = lax.dynamic_update_slice_in_dim(
+        jnp.zeros(lanes, z_in.dtype), z_in, newest * shaped, axis=0
+    )
+    frame_out = seen_now = z_in
+    for to_i in [*range(1, g_now // 2 + 1)]:
+        ledger = []
+        for it in [*range(g_now)]:
+            ledger.append((it, (it + 1) % g_now))
+        frame_out = lax.ppermute(frame_out, which_axis, ledger)
+        current_block = lax.dynamic_update_slice_in_dim(
+            current_block, frame_out, (newest - to_i) % g_now * shaped, axis=0
+        )
+        if 2 * to_i < g_now:
+            samples = []
+            for it in [*range(g_now)]:
+                samples.append((it, (it - 1) % g_now))
+            seen_now = lax.ppermute(seen_now, which_axis, samples)
+            current_block = lax.dynamic_update_slice_in_dim(
+                current_block, seen_now, (newest + to_i) % g_now * shaped, axis=0
+            )
+    return current_block
 
 
 def outer_step(master, moment, summed, groups):
@@ -79,7 +107,7 @@
         lax.all_gather(up_piece, ("replica", "shard"), axis=0, tiled=True),
         lax.all_gather(down_piece, ("replica", "shard"), axis=0, tiled=True),
     )
-    recast_embed = lax.all_gather(stored_rows.astype(jnp.bfloat16), "replica", axis=0, tiled=True)
+    recast_embed = _pack_boxes(stored_rows.astype(jnp.bfloat16), "replica")
     return (
         recast_up,
         recast_down,

time: 377 us -> 342 us (0.907)
  waiting for transfers between devices: 316 us -> 271 us
  blocking collectives: 23 us -> 32.3 us
    all_gather x1, waiting for transfers between devices: 108 us -> 72.1 us  [body(): lax.all_gather(up_piece, ('replica', 'shard'), axis=0, tiled=True)]
    all_gather x1 -> x0, waiting for transfers between devices: 25 us -> none  [body(): lax.all_gather(stored_rows.astype(jnp.bfloat16), 'replica', axis=0, tiled...]
    ppermute x0 -> x3, waiting for transfers between devices: none -> 10.6 us  [the longest x1 10.6 us: _pack_boxes(): seen_now = lax.ppermute(seen_now, which_axis, samples)]
    psum x1, blocking collectives: 6.93 us -> 16.2 us  [body(): norm_summed = lax.psum(trained_norm[0].astype(jnp.float32), 'replica')]
    unnamed x7 -> x6, waiting for transfers between devices: 38.1 us -> 42.5 us
    unnamed x30 -> x27, local copies, waits for them, and re-layouts: 10 us -> 7.6 us
  transfers between devices with their start and end apart: 6 -> 8, of which waited for: 6 -> 6; matrix products, arithmetic and copies ran while one was open for 4% -> 4% of each run, Pallas kernels for 0% -> 0%
where the time goes in v1:
time: 342 us; the launch traced here: 341 us
  waiting for transfers between devices  271 us (79%)
  blocking collectives  32.3 us (9%)
  between operations  14 us (4%)
  local copies, waits for them, and re-layouts  12.4 us (4%)
  other arithmetic  5.79 us (2%)
  matrix products  4.39 us (1%)
    all_gather x1, waiting for transfers between devices, body(): lax.all_gather(down_piece, ('replica', 'shard'), axis=0, tiled=True)  107 us
    all_gather x1, waiting for transfers between devices, body(): lax.all_gather(up_piece, ('replica', 'shard'), axis=0, tiled=True)  72.1 us
    unnamed x6, waiting for transfers between devices  42.5 us
    reduce_scatter x1, waiting for transfers between devices, body(): lax.psum_scatter(embed_terms.astype(jnp.bfloat16), 'replica', scatter_dim...  32.4 us
    psum x1, blocking collectives, body(): norm_summed = lax.psum(trained_norm[0].astype(jnp.float32), 'replica')  16.2 us
    ppermute x1, waiting for transfers between devices, _pack_boxes(): seen_now = lax.ppermute(seen_now, which_axis, samples)  10.6 us
    all_to_all x1, blocking collectives, body(): lax.all_to_all(up_summed, 'tensor', split_axis=1, concat_axis=3, tiled=True)  8.59 us
    unnamed x27, local copies, waits for them, and re-layouts  7.6 us
  transfers between devices with their start and end apart: 8, of which 6 were waited for; matrix products, arithmetic and copies ran while one was open for 4% of the time, Pallas kernels for 0%

profile of v1, /device:TPU:1, one launch (start us, length us, event | category | flops | bytes accessed | tf_op | source)
XLA Modules:
  0.0 341.3 jit_solution(16700294331705165196)
XLA Ops:
  7.2 0.0 all-reduce.3.cloned.1.call-start
  7.3 1.7 copy_bitcast_fusion
  9.0 0.0 reduce-scatter.4.cloned.1.call-start
  9.1 1.7 dynamic-slice_bitcast_fusion
  10.8 0.0 reduce-scatter.6.cloned.1.call-start
  10.8 0.7 reduce-scatter.6.cloned.1.call-update
  11.5 0.0 all-gather.4.cloned.1.call-start
  11.6 0.6 dynamic-slice
  12.2 41.8 %all-reduce.3.cloned.1.call-done = bf16[4,2,8,2048]{3,2,0,1:T(8,128)(2,1)} async-done(((bf16[4,2,8,2048]{3,2,0,1:T(8,128)(2,1)}), bf16[4,2,8,2048]{3,2,0,1:T(8,128)(2,1)}) %all-reduce.3.cloned.1.call-update) | async-done | bytes 262160
  54.0 1.5 dynamic-slice_convert_fusion
  55.5 8.6 %all_to_all.28 = f32[1,2,8,2048]{3,2,0,1:T(8,128)S(1)} all-to-all(f32[1,2,8,2048]{3,2,0,1:T(8,128)S(1)} %dynamic-slice_convert_fusion), channel_id=1, replica_groups=mesh['replica'=4,'shard'=16,'tensor'=2] {'tensor'}, dimensions={1} | all-to-all | bytes 262144 | tf_op jit(solution)/shard_map/all_to_all | solution.py:82
  64.1 0.7 fusion.15
  64.8 7.5 %all_to_all.29 = bf16[8,2,2048]{2,0,1:T(8,128)(2,1)} all-to-all(bf16[8,2,2048]{2,0,1:T(8,128)(2,1)S(1)} %bitcast.53), channel_id=1, replica_groups=mesh['replica'=4,'shard'=16,'tensor'=2] {'tensor'}, dimensions={1} | all-to-all | bytes 131072 | tf_op jit(solution)/shard_map/all_to_all | solution.py:102
  72.4 0.0 all-gather.4.cloned.1.call-update
  72.4 0.0 all-gather.6.cloned.1.call-start
  72.4 6.0 %reduce-scatter.4.cloned.1.call-done = bf16[1,32,1024]{2,1,0:T(8,128)(2,1)} async-done(((bf16[4,32,1024]{2,1,0:T(8,128)(2,1)}), bf16[1,32,1024]{2,1,0:T(8,128)(2,1)}) %reduce-scatter.4.cloned.1.call-update) | async-done | bytes 65552 | tf_op jit(solution)/shard_map/reduce_scatter | solution.py:75
  78.4 1.6 fusion.14
  80.0 32.4 %reduce-scatter.6.cloned.1.call-done = bf16[1,256,1024]{2,1,0:T(8,128)(2,1)} async-done(((bf16[4,256,1024]{2,1,0:T(8,128)(2,1)}), bf16[1,256,1024]{2,1,0:T(8,128)(2,1)}) %reduce-scatter.6.cloned.1.call-update) | async-done | bytes 524304 | tf_op jit(solution)/shard_map/reduce_scatter | solution.py:92
  112.4 2.2 fusion.1
  114.6 0.3 broadcast_in_dim.9
  114.9 2.2 constant_dynamic-update-slice_fusion.3
  117.1 16.2 %psum.7 = f32[2,1024]{1,0:T(2,128)S(1)} all-reduce(f32[2,1024]{1,0:T(2,128)S(1)} %bitcast_convert_fusion), channel_id=1, replica_groups=mesh['replica'=4,'shard'=16,'tensor'=2] {'replica'}, use_global_device_ids=true, to_apply=%region_3.4 | all-reduce | flops 2048 | bytes 16384 | tf_op jit(solution)/shard_map/psum | solution.py:87
  133.3 1.4 collective-permute-start.1
  134.7 0.1 collective-permute-start.2
  134.8 1.3 fusion.13
  136.1 0.6 fusion.8
  136.8 10.6 %collective-permute-done.1 = bf16[256,1024]{1,0:T(8,128)(2,1)} collective-permute-done((bf16[256,1024]{1,0:T(8,128)(2,1)}, bf16[256,1024]{1,0:T(8,128)(2,1)}, u32[]{:S(2)}, u32[]{:S(2)}) %collective-permute-start.1) | collective-permute-done | bytes 524320 | tf_op jit(solution)/shard_map/ppermute | solution.py:28
  147.4 1.1 constant_dynamic-update-slice_fusion.1
  148.6 72.1 %all-gather.4.cloned.1.call-done = bf16[1024,2048]{1,0:T(8,128)(2,1)} async-done(((bf16[16,2048]{1,0:T(8,128)(2,1)}), bf16[1024,2048]{1,0:T(8,128)(2,1)}) %all-gather.4.cloned.1.call-update) | async-done | bytes 4194320 | tf_op jit(solution)/shard_map/all_gather | solution.py:107
  220.7 107.2 %all-gather.6.cloned.1.call-done = bf16[1,2048,1024]{2,1,0:T(8,128)(2,1)} async-done(((bf16[1,32,1024]{2,1,0:T(8,128)(2,1)}), bf16[1,2048,1024]{2,1,0:T(8,128)(2,1)}) %all-gather.6.cloned.1.call-update) | async-done | bytes 4194320 | tf_op jit(solution)/shard_map/all_gather | solution.py:108
  327.9 4.9 %copy.42 = bf16[1024,2048]{1,0:T(8,128)(2,1)} copy(bf16[1024,2048]{1,0:T(8,128)(2,1)} %all-gather.4.cloned.1.call-done) | data formatting | bytes 8388608
  332.8 2.0 copy.43
  (34 shorter events, 0.2 us)
Async XLA Ops:
  7.2 105.2 %copy-start = (f32[1024,64]{0,1:T(8,128)S(1)}, f32[1024,64]{0,1:T(8,128)}, u32[]{:S(2)}) copy-start(f32[1024,64]{0,1:T(8,128)} %param.25) | copy-start | bytes 786436
  7.2 4.4 %copy-start.11 = (u32[128]{0:T(128)S(1)}, u32[128]{0:T(128)}, u32[]{:S(2)}) copy-start(u32[128]{0:T(128)} %constant.87) | copy-start | bytes 1540
  7.2 46.8 %all-reduce.3.cloned.1.call-start = ((), (), s32[]{:S(2)}) async-start(), calls=%async_computation.8 | async-start | bytes 524288
  7.3 56.8 %copy-start.7 = (f32[8,4096]{1,0:T(8,128)S(1)}, f32[8,4096]{1,0:T(8,128)}, u32[]{:S(2)}) copy-start(f32[8,4096]{1,0:T(8,128)} %param.17) | copy-start | bytes 393220
  7.3 56.8 %copy-start.8 = (f32[8,4096]{1,0:T(8,128)S(1)}, f32[8,4096]{1,0:T(8,128)}, u32[]{:S(2)}) copy-start(f32[8,4096]{1,0:T(8,128)} %param.18) | copy-start | bytes 393220
  9.0 69.4 %reduce-scatter.4.cloned.1.call-start = ((), (), s32[]{:S(2)}) async-start(), calls=%async_computation.5 | async-start | bytes 327680 | tf_op jit(solution)/shard_map/reduce_scatter | solution.py:75
  10.8 67.6 %copy-start.5 = (f32[1,32,1024]{2,1,0:T(8,128)S(1)}, f32[1,32,1024]{2,1,0:T(8,128)}, u32[]{:S(2)}) copy-start(f32[1,32,1024]{2,1,0:T(8,128)} %param.19) | copy-start | bytes 393220
  10.8 67.6 %copy-start.6 = (f32[1,32,1024]{2,1,0:T(8,128)S(1)}, f32[1,32,1024]{2,1,0:T(8,128)}, u32[]{:S(2)}) copy-start(f32[1,32,1024]{2,1,0:T(8,128)} %param.20) | copy-start | bytes 393220
  10.8 101.6 %reduce-scatter.6.cloned.1.call-start = ((), (), s32[]{:S(2)}) async-start(), calls=%async_computation.6 | async-start | bytes 2621440 | tf_op jit(solution)/shard_map/reduce_scatter | solution.py:92
  10.8 101.6 %copy-start.2 = (f32[1,256,1024]{2,1,0:T(8,128)S(1)}, f32[1,256,1024]{2,1,0:T(8,128)}, u32[]{:S(2)}) copy-start(f32[1,256,1024]{2,1,0:T(8,128)} %param.21) | copy-start | bytes 3145732
  11.5 209.2 %all-gather.4.cloned.1.call-start = ((), (), s32[]{:S(2)}) async-start(), calls=%async_computation.4 | async-start | bytes 4259840 | tf_op jit(solution)/shard_map/all_gather | solution.py:107
  72.4 255.5 %all-gather.6.cloned.1.call-start = ((), (), s32[]{:S(2)}) async-start(), calls=%async_computation.7 | async-start | bytes 4259840 | tf_op jit(solution)/shard_map/all_gather | solution.py:108
  80.0 34.8 %copy-start.4 = (f32[1,256,64]{1,2,0:T(8,128)S(1)}, f32[1,256,64]{1,2,0:T(8,128)}, u32[]{:S(2)}) copy-start(f32[1,256,64]{1,2,0:T(8,128)} %param.22) | copy-start | bytes 196612
  114.8 2.3 copy-start.10
  114.8 20.0 %copy-start.9 = (f32[2,1024]{1,0:T(2,128)S(1)}, f32[2,1024]{1,0:T(2,128)}, u32[]{:S(2)}) copy-start(f32[2,1024]{1,0:T(2,128)} %param.23) | copy-start | bytes 24580
  117.1 17.6 %collective-permute-start = (bf16[256,1024]{1,0:T(8,128)(2,1)}, bf16[256,1024]{1,0:T(8,128)(2,1)S(1)}, u32[]{:S(2)}, u32[]{:S(2)}) collective-permute-start(bf16[256,1024]{1,0:T(8,128)(2,1)} %get-tuple-element.16), channel_id=1, source_target_pairs={{0,32},{32,64},{64,96},{96,0},{1,33},{33,65},{65,97},{97,1},{2,34}... | collective-permute-start | bytes 1572872 | tf_op jit(solution)/shard_map/ppermute | solution.py:20
  133.3 14.1 %collective-permute-start.1 = (bf16[256,1024]{1,0:T(8,128)(2,1)}, bf16[256,1024]{1,0:T(8,128)(2,1)}, u32[]{:S(2)}, u32[]{:S(2)}) collective-permute-start(bf16[256,1024]{1,0:T(8,128)(2,1)} %get-tuple-element.16), channel_id=1, source_target_pairs={{0,96},{32,0},{64,32},{96,64},{1,97},{33,1},{65,33},{97,65},{2,98}... | collective-permute-start | bytes 1572872 | tf_op jit(solution)/shard_map/ppermute | solution.py:28
  134.7 13.8 %collective-permute-start.2 = (bf16[256,1024]{1,0:T(8,128)(2,1)S(1)}, bf16[256,1024]{1,0:T(8,128)(2,1)S(1)}, u32[]{:S(2)}, u32[]{:S(2)}) collective-permute-start(bf16[256,1024]{1,0:T(8,128)(2,1)S(1)} %collective-permute-done), channel_id=1, source_target_pairs={{0,32},{32,64},{64,96},{96,0},{1,33},{33,65},{65,97},{97,1},{2,34}... | collective-permute-start | bytes 1572872 | tf_op jit(solution)/shard_map/ppermute | solution.py:20
  148.5 184.3 %copy-start.3 = (bf16[1024,1024]{1,0:T(8,128)(2,1)}, bf16[1024,1024]{1,0:T(8,128)(2,1)S(1)}, u32[]{:S(2)}) copy-start(bf16[1024,1024]{1,0:T(8,128)(2,1)S(1)} %constant_dynamic-update-slice_fusion) | copy-start | bytes 6291460
  327.9 4.9 %copy-start.1 = (bf16[1,2048,1024]{2,1,0:T(8,128)(2,1)S(1)}, bf16[1,2048,1024]{2,1,0:T(8,128)(2,1)}, u32[]{:S(2)}) copy-start(bf16[1,2048,1024]{2,1,0:T(8,128)(2,1)} %all-gather.6.cloned.1.call-done) | copy-start | bytes 12582916
Sparse Core Ops, SparseCore 0:
  10.9 42.9 all-reduce.2
  57.0 21.2 reduce-scatter.3
  80.8 31.5 reduce-scatter.5
  114.1 106.5 all-gather.3
  222.9 104.8 all-gather.5
